TPU v7x, 32 devices: a whole 2x2x4 slice. The times are simulated.
32 devices in a mesh: row: 4 (over y, x), col: 8 (over z, core).
Axes of the slice: x: 2, y: 2, z: 4, core: 2. Of those that a mesh axis runs over, the one named last changes fastest.
Arguments:
- inputs: bfloat16 [2048, 25600], P('row', 'col'), may hold values from -6 to 6
- out_grads: bfloat16 [2048, 5120], P('col', 'row'), may hold values from -0.125 to 0.125
- weights: bfloat16 [5120, 25600], P('row', 'col'), may hold values from -3 to 3
- momentum: float32 [5120, 25600], P('row', 'col'), may hold values from -13 to 13
- right_factor: float32 [25600, 256], P('col'), may hold values from -6 to 6
Outputs:
- weights_new: float32 [5120, 25600], P('row', 'col')
- momentum_new: float32 [5120, 25600], P('row', 'col')
- factor_new: float32 [25600, 256], P('col')
All inputs are finite; a program needn't handle non-finite values.
Results may differ from a plain program's by a relative error of at most 0.0003.
Values may be sent and summed in bfloat16 or wider, within the bound.
No kernel may reach another device: no remote copies, remote signals or barrier semaphores. Data moves between devices by JAX's collectives and lax.ppermute only.
A program may use at most 128 MiB of HBM per device.

v0:
```python
import math
import jax
import jax.numpy as jnp
from jax import lax
from jax.sharding import PartitionSpec as P

M = 5120
N = 25600
RANK = 256
mix_rate = 0.95
step_rate = 0.3
weight_decay = 0.1
tiny_eps = 1e-06
highest = lax.Precision.HIGHEST


def inner_rows(left_side, right_in):
    return lax.dot_general(left_side, right_in, (((0,), (0,)), ((), ())), precision=highest)


def orthonormal(sketch_rows, gram_total):
    factor_low = jnp.linalg.cholesky(gram_total)
    return jax.scipy.linalg.solve_triangular(factor_low, sketch_rows.T, lower=True).T


def on_device(inputs, out_grads, weights, momentum, right_factor):
    grads_all = lax.all_gather(out_grads, "col", axis=0, tiled=True)
    gradient = lax.dot_general(
        grads_all,
        lax.all_gather(inputs, "row", axis=0, tiled=True),
        (((0,), (0,)), ((), ())),
        preferred_element_type=jnp.float32,
    )
    moment = momentum + gradient
    sketch_part = jnp.dot(moment, right_factor, precision=highest)
    sketch_rows = lax.psum(sketch_part, "col")
    gram_total = lax.psum(inner_rows(sketch_rows, sketch_rows), "row")
    basis_rows = orthonormal(sketch_rows, gram_total)
    right_part = inner_rows(moment, basis_rows)
    right_share = lax.psum_scatter(right_part, "row", scatter_dimension=0, tiled=True)
    squares = lax.psum(jnp.sum(right_share * right_share, axis=0), ("row", "col"))
    right_side = lax.all_gather(right_share, "row", axis=0, tiled=True)
    column_scale = lax.rsqrt(squares / N + tiny_eps)
    factor_new = right_side * column_scale
    momentum_new = moment - (1.0 - mix_rate) * jnp.dot(basis_rows, right_side.T, precision=highest)
    update = jnp.dot(basis_rows, factor_new.T, precision=highest)
    weights_new = (
        weights.astype(jnp.float32) * (1.0 - step_rate * weight_decay)
        - step_rate * math.sqrt(M / RANK) * update
    )
    return (weights_new, momentum_new, factor_new)


def solution(mesh):
    placed = (P("row", "col"), P("col", "row"), P("row", "col"), P("row", "col"), P("col", None))
    return jax.shard_map(
        on_device,
        mesh=mesh,
        in_specs=placed,
        out_specs=(P("row", "col"), P("row", "col"), P("col", None)),
        check_vma=False,
    )
```

profile of v0, /device:TPU:0, one launch (start us, length us, event | category | flops | bytes accessed | tf_op | source)
XLA Modules:
  0.0 616.2 jit_solution(3706774686516627048)
XLA Ops:
  7.2 0.0 copy-start
  7.2 0.0 all-gather.4.cloned.1.call-start
  7.2 0.7 all-gather.4.cloned.1.call-update
  7.9 0.0 all-gather.6.cloned.1.call-start
  8.0 0.7 all-gather.6.cloned.1.call-update
  8.7 0.0 all-reduce.4.cloned.1.call-start
  8.7 59.7 %all-gather.4.cloned.1.call-done = bf16[2048,1280]{1,0:T(8,128)(2,1)} async-done(((bf16[256,1280]{1,0:T(8,128)(2,1)}), bf16[2048,1280]{1,0:T(8,128)(2,1)}) %all-gather.4.cloned.1.call-update) | async-done | bytes 5242896 | tf_op jit(solution)/shard_map/all_gather | solution.py:27
  68.4 127.4 %all-gather.6.cloned.1.call-done = bf16[2048,3200]{1,0:T(8,128)(2,1)} async-done(((bf16[512,3200]{1,0:T(8,128)(2,1)}), bf16[2048,3200]{1,0:T(8,128)(2,1)}) %all-gather.6.cloned.1.call-update) | async-done | bytes 13107216 | tf_op jit(solution)/shard_map/all_gather | solution.py:30
  195.8 29.4 %convolution_add_fusion = f32[1280,3200]{1,0:T(8,128)} fusion(f32[1280,3200]{1,0:T(8,128)} %param.8, bf16[2048,1280]{1,0:T(8,128)(2,1)} %all-gather.4.cloned.1.call-done, bf16[2048,3200]{1,0:T(8,128)(2,1)} %all-gather.6.cloned.1.call-done), kind=kOutput, calls=%fused_computation.2 | convolution fusion | flops 16781312000 | bytes 51118080 | tf_op jit(solution)/shard_map/dot_general | solution.py:28
  225.1 17.8 %fusion.15 = f32[1280,256]{1,0:T(8,128)} fusion(f32[1280,3200]{1,0:T(8,128)} %convolution_add_fusion, f32[3200,256]{1,0:T(8,128)S(1)} %copy-done), kind=kOutput, calls=%fused_computation.41 | convolution fusion | flops 12582912000 | bytes 20971520 | tf_op jit(solution)/shard_map/dot_general | solution.py:35
  242.9 0.0 all-reduce.4.cloned.1.call-update
  242.9 0.0 all-reduce.6.cloned.1.call-start
  243.0 60.5 %all-reduce.4.cloned.1.call-done = f32[1280,256]{1,0:T(8,128)} async-done(((f32[1280,256]{1,0:T(8,128)}), f32[1280,256]{1,0:T(8,128)}) %all-reduce.4.cloned.1.call-update) | async-done | bytes 1310736 | tf_op jit(solution)/shard_map/psum | solution.py:36
  303.5 4.8 fusion.16
  308.3 0.0 all-reduce.6.cloned.1.call-update
  308.4 0.2 reduce-scatter.2.cloned.1.call-start
  308.6 42.0 %all-reduce.6.cloned.1.call-done = f32[256,256]{0,1:T(8,128)} async-done(((f32[256,256]{0,1:T(8,128)}), f32[256,256]{0,1:T(8,128)}) %all-reduce.6.cloned.1.call-update) | async-done | bytes 262160 | tf_op jit(solution)/shard_map/psum | solution.py:37
  350.6 1.1 copy.9
  351.7 1.0 fusion.5
  352.7 11.7 %cholesky.50 = f32[128,128]{1,0:T(8,128)S(1)} custom-call(f32[128,128]{1,0:T(8,128)S(1)} %cholesky.118), custom_call_target="Cholesky" | custom-call | tf_op jit(solution)/shard_map/jit(cholesky)/cholesky | solution.py:22
  364.4 9.8 %custom-call.15 = f32[1,128,128]{1,2,0:T(8,128)S(1)} custom-call(f32[1,128,128]{2,1,0:T(8,128)S(1)} %get-tuple-element.24), custom_call_target="InvertDiagBlocksLowerTriangular" | custom-call | tf_op jit(solution)/shard_map/jit(cholesky)/cholesky | solution.py:22
  374.3 0.2 constant_dynamic-update-slice_fusion.1
  374.5 0.3 convolution_subtract_fusion.1
  374.8 11.7 %cholesky.105 = f32[128,128]{1,0:T(8,128)S(1)} custom-call(f32[128,128]{1,0:T(8,128)S(1)} %convolution_subtract_fusion.1), custom_call_target="Cholesky" | custom-call | tf_op jit(solution)/shard_map/jit(cholesky)/cholesky | solution.py:22
  386.5 0.7 compare_reduce_fusion
  388.6 0.1 triangular_solve.57
  388.6 4.2 while.1
  388.8 0.6 fusion.31
  389.4 1.4 bitcast_dynamic-update-slice_fusion.2
  390.8 0.6 fusion.31
  391.4 1.4 bitcast_dynamic-update-slice_fusion.2
  392.8 19.7 %custom-call.16 = f32[2,128,128]{1,2,0:T(8,128)S(1)} custom-call(f32[2,128,128]{2,1,0:T(8,128)S(1)} %get-tuple-element.10), custom_call_target="InvertDiagBlocksLowerTriangular" | custom-call | tf_op jit(solution)/shard_map/jit(_solve_triangular)/triangular_solve | solution.py:23
  412.5 0.8 fusion.3
  413.3 1.2 convolution_subtract_fusion
  414.5 0.8 fusion.7
  415.2 0.0 copy-start.6
  415.2 32.1 %fusion.2 = f32[3200,256]{1,0:T(8,128)} fusion(f32[1280,3200]{1,0:T(8,128)} %convolution_add_fusion, f32[128,1280]{1,0:T(8,128)S(1)} %fusion.7, f32[128,1280]{1,0:T(8,128)S(1)} %fusion.3), kind=kOutput, calls=%fused_computation.11 | convolution fusion | flops 12583239680 | bytes 20971520 | tf_op jit(solution)/shard_map/dot_general | solution.py:18
  447.4 0.0 reduce-scatter.2.cloned.1.call-update
  447.4 0.0 all-gather.8.cloned.1.call-start
  447.4 45.1 %reduce-scatter.2.cloned.1.call-done = f32[800,256]{1,0:T(8,128)} async-done(((f32[3200,256]{1,0:T(8,128)}), f32[800,256]{1,0:T(8,128)}) %reduce-scatter.2.cloned.1.call-update) | async-done | bytes 819216 | tf_op jit(solution)/shard_map/reduce_scatter | solution.py:40
  492.5 0.0 all-gather.8.cloned.1.call-update
  492.6 1.3 multiply_reduce_fusion
  493.8 40.3 %psum.23 = f32[256]{0:T(256)S(1)} all-reduce(f32[256]{0:T(256)S(1)} %multiply_reduce_fusion), channel_id=1, replica_groups=mesh['row'=4,'col'=8] {'row','col'}, use_global_device_ids=true, to_apply=%region_8.9 | all-reduce | flops 256 | bytes 2048 | tf_op jit(solution)/shard_map/psum | solution.py:41
  534.1 6.0 all-gather.8.cloned.1.call-done
  540.1 2.1 broadcast_multiply_fusion
  542.2 0.0 copy-start.3
  542.3 32.8 %fusion.1 = f32[1280,3200]{1,0:T(8,128)} fusion(f32[3200,256]{1,0:T(8,128)S(1)} %broadcast_multiply_fusion, bf16[1280,3200]{1,0:T(8,128)(2,1)} %param.7, f32[128,1280]{1,0:T(8,128)S(1)} %fusion.7, f32[128,1280]{1,0:T(8,128)S(1)} %fusion.3), kind=kOutput, calls=%fused_computation.6 | convolution fusion | flops 12599623680 | bytes 29163520 | tf_op jit(solution)/shard_map/dot_general | solution.py:46
  575.0 34.1 %fusion = f32[1280,3200]{1,0:T(8,128)} fusion(f32[1280,3200]{1,0:T(8,128)} %convolution_add_fusion, f32[3200,256]{1,0:T(8,128)S(1)} %copy-done.4, f32[128,1280]{1,0:T(8,128)} %copy-done.6, f32[128,1280]{1,0:T(8,128)} %copy-done.2), kind=kOutput, calls=%fused_computation.4 | convolution fusion | flops 12591431680 | bytes 37355520 | tf_op jit(solution)/shard_map/dot_general | solution.py:45
  (21 shorter events, 0.2 us)
Async XLA Ops:
  7.2 217.9 %copy-start = (f32[3200,256]{1,0:T(8,128)S(1)}, f32[3200,256]{1,0:T(8,128)}, u32[]{:S(2)}) copy-start(f32[3200,256]{1,0:T(8,128)} %param.9) | copy-start | bytes 9830404
  7.2 61.2 %all-gather.4.cloned.1.call-start = ((), (), s32[]{:S(2)}) async-start(), calls=%async_computation.1 | async-start | bytes 5898240 | tf_op jit(solution)/shard_map/all_gather | solution.py:27
  7.9 187.8 %all-gather.6.cloned.1.call-start = ((), (), s32[]{:S(2)}) async-start(), calls=%async_computation.2 | async-start | bytes 16384000 | tf_op jit(solution)/shard_map/all_gather | solution.py:30
  8.7 294.8 %all-reduce.4.cloned.1.call-start = ((), (), s32[]{:S(2)}) async-start(), calls=%async_computation.3 | async-start | bytes 2621440 | tf_op jit(solution)/shard_map/psum | solution.py:36
  242.9 107.7 %all-reduce.6.cloned.1.call-start = ((), (), s32[]{:S(2)}) async-start(), calls=%async_computation.4 | async-start | bytes 524288 | tf_op jit(solution)/shard_map/psum | solution.py:37
  303.5 109.0 %copy-start.5 = (f32[1280,256]{1,0:T(8,128)S(1)}, f32[1280,256]{1,0:T(8,128)}, u32[]{:S(2)}) copy-start(f32[1280,256]{1,0:T(8,128)} %all-reduce.4.cloned.1.call-done) | copy-start | bytes 3932164
  308.4 184.2 %reduce-scatter.2.cloned.1.call-start = ((), (), s32[]{:S(2)}) async-start(), calls=%async_computation.5 | async-start | bytes 4096000 | tf_op jit(solution)/shard_map/reduce_scatter | solution.py:40
  413.3 129.0 %copy-start.2 = (f32[128,1280]{1,0:T(8,128)}, f32[128,1280]{1,0:T(8,128)S(1)}, u32[]{:S(2)}) copy-start(f32[128,1280]{1,0:T(8,128)S(1)} %fusion.3) | copy-start | bytes 1966084
  415.2 127.0 %copy-start.6 = (f32[128,1280]{1,0:T(8,128)}, f32[128,1280]{1,0:T(8,128)S(1)}, u32[]{:S(2)}) copy-start(f32[128,1280]{1,0:T(8,128)S(1)} %fusion.7) | copy-start | bytes 1966084
  447.4 92.7 %all-gather.8.cloned.1.call-start = ((), (), s32[]{:S(2)}) async-start(), calls=%async_computation.6 | async-start | bytes 4096000 | tf_op jit(solution)/shard_map/all_gather | solution.py:42
  542.2 32.8 %copy-start.3 = (f32[3200,256]{1,0:T(8,128)}, f32[3200,256]{1,0:T(8,128)S(1)}, u32[]{:S(2)}) copy-start(f32[3200,256]{1,0:T(8,128)S(1)} %broadcast_multiply_fusion) | copy-start | bytes 9830404
  542.3 32.8 %copy-start.4 = (f32[3200,256]{1,0:T(8,128)S(1)}, f32[3200,256]{1,0:T(8,128)}, u32[]{:S(2)}) copy-start(f32[3200,256]{1,0:T(8,128)} %all-gather.8.cloned.1.call-done) | copy-start | bytes 9830404
  575.0 34.1 %copy-start.1 = (f32[3200,256]{1,0:T(8,128)S(1)}, f32[3200,256]{1,0:T(8,128)}, u32[]{:S(2)}) copy-start(f32[3200,256]{1,0:T(8,128)} %param.9) | copy-start | bytes 9830404
Sparse Core Ops, SparseCore 0:
  9.6 58.6 all-gather.3
  70.2 125.5 all-gather.5
  243.0 60.4 all-reduce.3
  308.5 42.0 all-reduce.5
  447.5 44.9 reduce-scatter.1
  494.2 45.7 all-gather.7
where the time goes:
time: 623 us; the launch traced here: 616 us
  waiting for transfers between devices  342 us (55%)
  matrix products  154 us (25%)
  other arithmetic  58.1 us (9%)
  blocking collectives  40.3 us (6%)
  between operations  15.8 us (3%)
    all_gather x1, waiting for transfers between devices, on_device(): lax.all_gather(inputs, 'row', axis=0, tiled=True)  127 us
    psum x1, waiting for transfers between devices, on_device(): sketch_rows = lax.psum(sketch_part, 'col')  60.5 us
    all_gather x1, waiting for transfers between devices, on_device(): grads_all = lax.all_gather(out_grads, 'col', axis=0, tiled=True)  59.7 us
    reduce_scatter x1, waiting for transfers between devices, on_device(): lax.psum_scatter(right_part, 'row', scatter_dimension=0, tiled=True)  45.1 us
    psum x1, waiting for transfers between devices, on_device(): gram_total = lax.psum(inner_rows(sketch_rows, sketch_rows), 'row')  42 us
    psum x1, blocking collectives, on_device(): lax.psum(jnp.sum(right_share * right_share, axis=0), ('row', 'col'))  40.3 us
    dot_general x2, matrix products, inner_rows(): lax.dot_general(left_side, right_in, (((0,), (0,)), ((), ())), precision=...  36.9 us
    dot_general x1, matrix products, on_device(): jnp.dot(basis_rows, right_side.T, precision=highest)  34.1 us
  transfers between devices with their start and end apart: 6, of which 6 were waited for; matrix products, arithmetic and copies ran while one was open for 0% of the time, Pallas kernels for 0%

commit v1 on v0

--- a/solution.py
+++ b/solution.py
@@ -24,7 +24,12 @@
 
 
 def on_device(inputs, out_grads, weights, momentum, right_factor):
-    grads_all = lax.all_gather(out_grads, "col", axis=0, tiled=True)
+    ring = [out_grads]
+    for hop in range(7):
+        ring.append(lax.ppermute(ring[-1], "col", [(dev, (dev + 1) % 8) for dev in range(8)]))
+    grads_all = jnp.roll(
+        jnp.concatenate(ring[::-1], axis=0), (lax.axis_index("col") + 1) * ring[0].shape[0], axis=0
+    )
     gradient = lax.dot_general(
         grads_all,
         lax.all_gather(inputs, "row", axis=0, tiled=True),

time: 623 us -> 581 us (0.933)
  waiting for transfers between devices: 342 us -> 256 us
  local copies, waits for them, and re-layouts: 5.14 us -> 34.3 us
  matrix products: 154 us -> 167 us
    all_gather x1, waiting for transfers between devices: 127 us -> 17.9 us  [on_device(): lax.all_gather(inputs, 'row', axis=0, tiled=True)]
    ppermute x0 -> x7, waiting for transfers between devices: none -> 83.7 us  [on_device(): lax.ppermute(ring[-1], 'col', [(dev, (dev + 1) % 8) for dev in range(8)])]
    all_gather x1 -> x0, waiting for transfers between devices: 59.7 us -> none  [on_device(): grads_all = lax.all_gather(out_grads, 'col', axis=0, tiled=True)]
    unnamed x14 -> x49, local copies, waits for them, and re-layouts: 0.04 us -> 28.3 us
    dot_general x1, matrix products: 17.8 us -> 28.8 us  [on_device(): sketch_part = jnp.dot(moment, right_factor, precision=highest)]
  transfers between devices with their start and end apart: 6 -> 12, of which waited for: 6 -> 12; matrix products, arithmetic and copies ran while one was open for 0% -> 5% of each run, Pallas kernels for 0% -> 0%
where the time goes in v1:
time: 581 us; the launch traced here: 573 us
  waiting for transfers between devices  256 us (44%)
  matrix products  167 us (29%)
  other arithmetic  58.1 us (10%)
  blocking collectives  40.3 us (7%)
  local copies, waits for them, and re-layouts  34.3 us (6%)
  between operations  15.5 us (3%)
    ppermute x7, waiting for transfers between devices, on_device(): lax.ppermute(ring[-1], 'col', [(dev, (dev + 1) % 8) for dev in range(8)])  83.7 us
    psum x1, waiting for transfers between devices, on_device(): sketch_rows = lax.psum(sketch_part, 'col')  60.5 us
    reduce_scatter x1, waiting for transfers between devices, on_device(): lax.psum_scatter(right_part, 'row', scatter_dimension=0, tiled=True)  45.1 us
    psum x1, waiting for transfers between devices, on_device(): gram_total = lax.psum(inner_rows(sketch_rows, sketch_rows), 'row')  42.2 us
    psum x1, blocking collectives, on_device(): lax.psum(jnp.sum(right_share * right_share, axis=0), ('row', 'col'))  40.3 us
    dot_general x2, matrix products, inner_rows(): lax.dot_general(left_side, right_in, (((0,), (0,)), ((), ())), precision=...  36.5 us
    dot_general x1, matrix products, on_device(): jnp.dot(basis_rows, right_side.T, precision=highest)  34.2 us
    another operation x6, other arithmetic, orthonormal(): factor_low = jnp.linalg.cholesky(gram_total)  33.9 us
  transfers between devices with their start and end apart: 12, of which 12 were waited for; matrix products, arithmetic and copies ran while one was open for 5% of the time, Pallas kernels for 0%

profile of v1, /device:TPU:0, one launch (start us, length us, event | category | flops | bytes accessed | tf_op | source)
XLA Modules:
  0.0 572.6 jit_solution(720878356198002838)
XLA Ops:
  8.5 12.5 %collective-permute-done = bf16[256,1280]{1,0:T(8,128)(2,1)S(1)} collective-permute-done((bf16[256,1280]{1,0:T(8,128)(2,1)}, bf16[256,1280]{1,0:T(8,128)(2,1)S(1)}, u32[]{:S(2)}, u32[]{:S(2)}) %collective-permute-start) | collective-permute-done | bytes 655392 | tf_op jit(solution)/shard_map/ppermute | solution.py:29
  21.9 11.8 %collective-permute-done.1 = bf16[256,1280]{1,0:T(8,128)(2,1)S(1)} collective-permute-done((bf16[256,1280]{1,0:T(8,128)(2,1)S(1)}, bf16[256,1280]{1,0:T(8,128)(2,1)S(1)}, u32[]{:S(2)}, u32[]{:S(2)}) %collective-permute-start.1) | collective-permute-done | bytes 655392 | tf_op jit(solution)/shard_map/ppermute | solution.py:29
  34.5 11.8 %collective-permute-done.2 = bf16[256,1280]{1,0:T(8,128)(2,1)S(1)} collective-permute-done((bf16[256,1280]{1,0:T(8,128)(2,1)S(1)}, bf16[256,1280]{1,0:T(8,128)(2,1)S(1)}, u32[]{:S(2)}, u32[]{:S(2)}) %collective-permute-start.2) | collective-permute-done | bytes 655392 | tf_op jit(solution)/shard_map/ppermute | solution.py:29
  47.2 11.8 %collective-permute-done.3 = bf16[256,1280]{1,0:T(8,128)(2,1)S(1)} collective-permute-done((bf16[256,1280]{1,0:T(8,128)(2,1)S(1)}, bf16[256,1280]{1,0:T(8,128)(2,1)S(1)}, u32[]{:S(2)}, u32[]{:S(2)}) %collective-permute-start.3) | collective-permute-done | bytes 655392 | tf_op jit(solution)/shard_map/ppermute | solution.py:29
  59.8 11.8 %collective-permute-done.4 = bf16[256,1280]{1,0:T(8,128)(2,1)S(1)} collective-permute-done((bf16[256,1280]{1,0:T(8,128)(2,1)S(1)}, bf16[256,1280]{1,0:T(8,128)(2,1)S(1)}, u32[]{:S(2)}, u32[]{:S(2)}) %collective-permute-start.4) | collective-permute-done | bytes 655392 | tf_op jit(solution)/shard_map/ppermute | solution.py:29
  72.5 11.9 %collective-permute-done.5 = bf16[256,1280]{1,0:T(8,128)(2,1)} collective-permute-done((bf16[256,1280]{1,0:T(8,128)(2,1)S(1)}, bf16[256,1280]{1,0:T(8,128)(2,1)}, u32[]{:S(2)}, u32[]{:S(2)}) %collective-permute-start.5) | collective-permute-done | bytes 655392 | tf_op jit(solution)/shard_map/ppermute | solution.py:29
  84.4 12.1 %collective-permute-done.6 = bf16[256,1280]{1,0:T(8,128)(2,1)} collective-permute-done((bf16[256,1280]{1,0:T(8,128)(2,1)}, bf16[256,1280]{1,0:T(8,128)(2,1)}, u32[]{:S(2)}, u32[]{:S(2)}) %collective-permute-start.6) | collective-permute-done | bytes 655392 | tf_op jit(solution)/shard_map/ppermute | solution.py:29
  96.5 2.0 constant_dynamic-update-slice_fusion.15
  98.5 2.0 constant_dynamic-update-slice_fusion.14
  100.5 2.0 constant_dynamic-update-slice_fusion.13
  102.4 2.0 constant_dynamic-update-slice_fusion.12
  104.4 2.0 constant_dynamic-update-slice_fusion.11
  106.4 2.0 constant_dynamic-update-slice_fusion.10
  108.3 2.0 constant_dynamic-update-slice_fusion.9
  110.3 2.0 constant_dynamic-update-slice_fusion.8
  112.2 2.0 constant_dynamic-update-slice_fusion.7
  114.2 2.0 constant_dynamic-update-slice_fusion.6
  116.2 0.9 constant_dynamic-update-slice_fusion.5
  117.1 0.9 constant_dynamic-update-slice_fusion.4
  117.9 0.9 constant_dynamic-update-slice_fusion.3
  118.8 0.9 constant_dynamic-update-slice_fusion.2
  119.7 0.9 constant_dynamic-update-slice_fusion.1
  120.6 0.9 constant_dynamic-update-slice_fusion
  121.5 17.9 %all-gather.3.cloned.1.call-done = bf16[2048,3200]{1,0:T(8,128)(2,1)} async-done(((bf16[512,3200]{1,0:T(8,128)(2,1)}), bf16[2048,3200]{1,0:T(8,128)(2,1)}) %all-gather.3.cloned.1.call-update) | async-done | bytes 13107216 | tf_op jit(solution)/shard_map/all_gather | solution.py:35
  139.3 29.4 %convolution_add_fusion = f32[1280,3200]{1,0:T(8,128)} fusion(f32[1280,3200]{1,0:T(8,128)} %param.8, bf16[2048,3200]{1,0:T(8,128)(2,1)} %all-gather.3.cloned.1.call-done, bf16[4096,1280]{1,0:T(8,128)(2,1)} %constant_dynamic-update-slice_fusion, s32[]{:T(128)S(6)} %select_n.18), kind=kOutput, calls=%fused_computation.2 | convolution fusion | flops 16781312000 | bytes 51118084 | tf_op jit(solution)/shard_map/dot_general | solution.py:33
  168.7 28.8 %fusion.17 = f32[1280,256]{1,0:T(8,128)} fusion(f32[1280,3200]{1,0:T(8,128)} %convolution_add_fusion, f32[3200,256]{1,0:T(8,128)S(1)} %copy-done), kind=kOutput, calls=%fused_computation.59 | convolution fusion | flops 12582912000 | bytes 20971520 | tf_op jit(solution)/shard_map/dot_general | solution.py:40
  197.6 60.5 %all-reduce.4.cloned.1.call-done = f32[1280,256]{1,0:T(8,128)} async-done(((f32[1280,256]{1,0:T(8,128)}), f32[1280,256]{1,0:T(8,128)}) %all-reduce.4.cloned.1.call-update) | async-done | bytes 1310736 | tf_op jit(solution)/shard_map/psum | solution.py:41
  258.1 4.6 fusion.18
  262.9 42.2 %all-reduce.6.cloned.1.call-done = f32[256,256]{0,1:T(8,128)} async-done(((f32[256,256]{0,1:T(8,128)}), f32[256,256]{0,1:T(8,128)}) %all-reduce.6.cloned.1.call-update) | async-done | bytes 262160 | tf_op jit(solution)/shard_map/psum | solution.py:42
  305.0 1.1 copy.9
  306.1 1.0 fusion.6
  307.1 11.7 %cholesky.50 = f32[128,128]{1,0:T(8,128)S(1)} custom-call(f32[128,128]{1,0:T(8,128)S(1)} %cholesky.118), custom_call_target="Cholesky" | custom-call | tf_op jit(solution)/shard_map/jit(cholesky)/cholesky | solution.py:22
  318.9 9.8 %custom-call.15 = f32[1,128,128]{1,2,0:T(8,128)S(1)} custom-call(f32[1,128,128]{2,1,0:T(8,128)S(1)} %get-tuple-element.24), custom_call_target="InvertDiagBlocksLowerTriangular" | custom-call | tf_op jit(solution)/shard_map/jit(cholesky)/cholesky | solution.py:22
  329.2 11.7 %cholesky.105 = f32[128,128]{1,0:T(8,128)S(1)} custom-call(f32[128,128]{1,0:T(8,128)S(1)} %convolution_subtract_fusion.1), custom_call_target="Cholesky" | custom-call | tf_op jit(solution)/shard_map/jit(cholesky)/cholesky | solution.py:22
  343.0 4.4 while.1
  344.0 1.4 bitcast_dynamic-update-slice_fusion.2
  346.0 1.4 bitcast_dynamic-update-slice_fusion.2
  347.4 19.7 %custom-call.16 = f32[2,128,128]{1,2,0:T(8,128)S(1)} custom-call(f32[2,128,128]{2,1,0:T(8,128)S(1)} %get-tuple-element.10), custom_call_target="InvertDiagBlocksLowerTriangular" | custom-call | tf_op jit(solution)/shard_map/jit(_solve_triangular)/triangular_solve | solution.py:23
  367.1 1.8 fusion.4
  368.9 2.5 convolution_subtract_fusion
  372.2 31.8 %fusion.3 = f32[3200,256]{1,0:T(8,128)} fusion(f32[1280,3200]{1,0:T(8,128)} %convolution_add_fusion, f32[128,1280]{1,0:T(8,128)S(1)} %fusion.8, f32[128,1280]{1,0:T(8,128)S(1)} %fusion.4), kind=kOutput, calls=%fused_computation.12 | convolution fusion | flops 12583239680 | bytes 20971520 | tf_op jit(solution)/shard_map/dot_general | solution.py:18
  404.1 45.1 %reduce-scatter.2.cloned.1.call-done = f32[800,256]{1,0:T(8,128)} async-done(((f32[3200,256]{1,0:T(8,128)}), f32[800,256]{1,0:T(8,128)}) %reduce-scatter.2.cloned.1.call-update) | async-done | bytes 819216 | tf_op jit(solution)/shard_map/reduce_scatter | solution.py:45
  449.2 1.3 multiply_reduce_fusion
  450.5 40.3 %psum.23 = f32[256]{0:T(256)S(1)} all-reduce(f32[256]{0:T(256)S(1)} %multiply_reduce_fusion), channel_id=1, replica_groups=mesh['row'=4,'col'=8] {'row','col'}, use_global_device_ids=true, to_apply=%region_8.9 | all-reduce | flops 256 | bytes 2048 | tf_op jit(solution)/shard_map/psum | solution.py:46
  490.8 5.9 %all-gather.5.cloned.1.call-done = f32[3200,256]{1,0:T(8,128)} async-done(((f32[800,256]{1,0:T(8,128)}), f32[3200,256]{1,0:T(8,128)}) %all-gather.5.cloned.1.call-update) | async-done | bytes 3276816 | tf_op jit(solution)/shard_map/all_gather | solution.py:47
  496.7 2.1 broadcast_multiply_fusion
  498.9 32.8 %fusion.1 = f32[1280,3200]{1,0:T(8,128)} fusion(f32[3200,256]{1,0:T(8,128)S(1)} %broadcast_multiply_fusion, bf16[1280,3200]{1,0:T(8,128)(2,1)} %param.7, f32[128,1280]{1,0:T(8,128)S(1)} %fusion.8, f32[128,1280]{1,0:T(8,128)S(1)} %fusion.4), kind=kOutput, calls=%fused_computation.6 | convolution fusion | flops 12599623680 | bytes 29163520 | tf_op jit(solution)/shard_map/dot_general | solution.py:51
  531.7 34.2 %fusion = f32[1280,3200]{1,0:T(8,128)} fusion(f32[1280,3200]{1,0:T(8,128)} %convolution_add_fusion, f32[3200,256]{1,0:T(8,128)S(1)} %copy-done.4, f32[128,1280]{1,0:T(8,128)} %copy-done.5, f32[128,1280]{1,0:T(8,128)} %copy-done.2), kind=kOutput, calls=%fused_computation.4 | convolution fusion | flops 12591431680 | bytes 37355520 | tf_op jit(solution)/shard_map/dot_general | solution.py:50
  (68 shorter events, 9.1 us)
Async XLA Ops:
  7.2 161.5 %copy-start = (f32[3200,256]{1,0:T(8,128)S(1)}, f32[3200,256]{1,0:T(8,128)}, u32[]{:S(2)}) copy-start(f32[3200,256]{1,0:T(8,128)} %param.9) | copy-start | bytes 9830404
  7.2 132.2 %all-gather.3.cloned.1.call-start = ((), (), s32[]{:S(2)}) async-start(), calls=%async_computation.1 | async-start | bytes 16384000 | tf_op jit(solution)/shard_map/all_gather | solution.py:35
  7.9 250.2 %all-reduce.4.cloned.1.call-start = ((), (), s32[]{:S(2)}) async-start(), calls=%async_computation.2 | async-start | bytes 2621440 | tf_op jit(solution)/shard_map/psum | solution.py:41
  8.0 13.1 %collective-permute-start = (bf16[256,1280]{1,0:T(8,128)(2,1)}, bf16[256,1280]{1,0:T(8,128)(2,1)S(1)}, u32[]{:S(2)}, u32[]{:S(2)}) collective-permute-start(bf16[256,1280]{1,0:T(8,128)(2,1)} %param.6), channel_id=1, source_target_pairs={{0,1},{1,2},{2,3},{3,4},{4,5},{5,6},{6,7},{7,0},{8,9},{9,10},{10,1... | collective-permute-start | bytes 1966088 | tf_op jit(solution)/shard_map/ppermute | solution.py:29
  21.0 0.9 copy-start.7
  21.9 11.8 %collective-permute-start.1 = (bf16[256,1280]{1,0:T(8,128)(2,1)S(1)}, bf16[256,1280]{1,0:T(8,128)(2,1)S(1)}, u32[]{:S(2)}, u32[]{:S(2)}) collective-permute-start(bf16[256,1280]{1,0:T(8,128)(2,1)S(1)} %collective-permute-done), channel_id=1, source_target_pairs={{0,1},{1,2},{2,3},{3,4},{4,5},{5,6},{6,7},{7,0},{8,9},{9,10},{10,1... | collective-permute-start | bytes 1966088 | tf_op jit(solution)/shard_map/ppermute | solution.py:29
  33.7 0.9 copy-start.9
  34.5 11.8 %collective-permute-start.2 = (bf16[256,1280]{1,0:T(8,128)(2,1)S(1)}, bf16[256,1280]{1,0:T(8,128)(2,1)S(1)}, u32[]{:S(2)}, u32[]{:S(2)}) collective-permute-start(bf16[256,1280]{1,0:T(8,128)(2,1)S(1)} %collective-permute-done.1), channel_id=1, source_target_pairs={{0,1},{1,2},{2,3},{3,4},{4,5},{5,6},{6,7},{7,0},{8,9},{9,10},{10,1... | collective-permute-start | bytes 1966088 | tf_op jit(solution)/shard_map/ppermute | solution.py:29
  46.3 0.9 copy-start.11
  47.2 11.8 %collective-permute-start.3 = (bf16[256,1280]{1,0:T(8,128)(2,1)S(1)}, bf16[256,1280]{1,0:T(8,128)(2,1)S(1)}, u32[]{:S(2)}, u32[]{:S(2)}) collective-permute-start(bf16[256,1280]{1,0:T(8,128)(2,1)S(1)} %collective-permute-done.2), channel_id=1, source_target_pairs={{0,1},{1,2},{2,3},{3,4},{4,5},{5,6},{6,7},{7,0},{8,9},{9,10},{10,1... | collective-permute-start | bytes 1966088 | tf_op jit(solution)/shard_map/ppermute | solution.py:29
  59.0 0.8 copy-start.13
  59.8 11.8 %collective-permute-start.4 = (bf16[256,1280]{1,0:T(8,128)(2,1)S(1)}, bf16[256,1280]{1,0:T(8,128)(2,1)S(1)}, u32[]{:S(2)}, u32[]{:S(2)}) collective-permute-start(bf16[256,1280]{1,0:T(8,128)(2,1)S(1)} %collective-permute-done.3), channel_id=1, source_target_pairs={{0,1},{1,2},{2,3},{3,4},{4,5},{5,6},{6,7},{7,0},{8,9},{9,10},{10,1... | collective-permute-start | bytes 1966088 | tf_op jit(solution)/shard_map/ppermute | solution.py:29
  71.7 0.8 copy-start.15
  72.5 11.9 %collective-permute-start.5 = (bf16[256,1280]{1,0:T(8,128)(2,1)S(1)}, bf16[256,1280]{1,0:T(8,128)(2,1)}, u32[]{:S(2)}, u32[]{:S(2)}) collective-permute-start(bf16[256,1280]{1,0:T(8,128)(2,1)S(1)} %collective-permute-done.4), channel_id=1, source_target_pairs={{0,1},{1,2},{2,3},{3,4},{4,5},{5,6},{6,7},{7,0},{8,9},{9,10},{10,1... | collective-permute-start | bytes 1966088 | tf_op jit(solution)/shard_map/ppermute | solution.py:29
  84.4 12.1 %collective-permute-start.6 = (bf16[256,1280]{1,0:T(8,128)(2,1)}, bf16[256,1280]{1,0:T(8,128)(2,1)}, u32[]{:S(2)}, u32[]{:S(2)}) collective-permute-start(bf16[256,1280]{1,0:T(8,128)(2,1)} %collective-permute-done.5), channel_id=1, source_target_pairs={{0,1},{1,2},{2,3},{3,4},{4,5},{5,6},{6,7},{7,0},{8,9},{9,10},{10,1... | collective-permute-start | bytes 1966088 | tf_op jit(solution)/shard_map/ppermute | solution.py:29
  84.4 31.8 %copy-start.16 = (bf16[256,1280]{1,0:T(8,128)(2,1)S(1)}, bf16[256,1280]{1,0:T(8,128)(2,1)}, u32[]{:S(2)}) copy-start(bf16[256,1280]{1,0:T(8,128)(2,1)} %copy-done.15) | copy-start | bytes 1966084
  84.4 32.7 %copy-start.14 = (bf16[256,1280]{1,0:T(8,128)(2,1)S(1)}, bf16[256,1280]{1,0:T(8,128)(2,1)}, u32[]{:S(2)}) copy-start(bf16[256,1280]{1,0:T(8,128)(2,1)} %copy-done.13) | copy-start | bytes 1966084
  84.4 33.5 %copy-start.12 = (bf16[256,1280]{1,0:T(8,128)(2,1)S(1)}, bf16[256,1280]{1,0:T(8,128)(2,1)}, u32[]{:S(2)}) copy-start(bf16[256,1280]{1,0:T(8,128)(2,1)} %copy-done.11) | copy-start | bytes 1966084
  84.4 34.4 %copy-start.10 = (bf16[256,1280]{1,0:T(8,128)(2,1)S(1)}, bf16[256,1280]{1,0:T(8,128)(2,1)}, u32[]{:S(2)}) copy-start(bf16[256,1280]{1,0:T(8,128)(2,1)} %copy-done.9) | copy-start | bytes 1966084
  84.4 35.3 %copy-start.8 = (bf16[256,1280]{1,0:T(8,128)(2,1)S(1)}, bf16[256,1280]{1,0:T(8,128)(2,1)}, u32[]{:S(2)}) copy-start(bf16[256,1280]{1,0:T(8,128)(2,1)} %copy-done.7) | copy-start | bytes 1966084
  84.4 36.2 %copy-start.6 = (bf16[256,1280]{1,0:T(8,128)(2,1)S(1)}, bf16[256,1280]{1,0:T(8,128)(2,1)}, u32[]{:S(2)}) copy-start(bf16[256,1280]{1,0:T(8,128)(2,1)} %param.6) | copy-start | bytes 1966084
  197.5 107.5 %all-reduce.6.cloned.1.call-start = ((), (), s32[]{:S(2)}) async-start(), calls=%async_computation.3 | async-start | bytes 524288 | tf_op jit(solution)/shard_map/psum | solution.py:42
  262.8 186.4 %reduce-scatter.2.cloned.1.call-start = ((), (), s32[]{:S(2)}) async-start(), calls=%async_computation.4 | async-start | bytes 4096000 | tf_op jit(solution)/shard_map/reduce_scatter | solution.py:45
  368.9 130.0 %copy-start.2 = (f32[128,1280]{1,0:T(8,128)}, f32[128,1280]{1,0:T(8,128)S(1)}, u32[]{:S(2)}) copy-start(f32[128,1280]{1,0:T(8,128)S(1)} %fusion.4) | copy-start | bytes 1966084
  372.2 126.7 %copy-start.5 = (f32[128,1280]{1,0:T(8,128)}, f32[128,1280]{1,0:T(8,128)S(1)}, u32[]{:S(2)}) copy-start(f32[128,1280]{1,0:T(8,128)S(1)} %fusion.8) | copy-start | bytes 1966084
  404.1 92.7 %all-gather.5.cloned.1.call-start = ((), (), s32[]{:S(2)}) async-start(), calls=%async_computation.5 | async-start | bytes 4096000 | tf_op jit(solution)/shard_map/all_gather | solution.py:47
  498.9 32.8 %copy-start.3 = (f32[3200,256]{1,0:T(8,128)}, f32[3200,256]{1,0:T(8,128)S(1)}, u32[]{:S(2)}) copy-start(f32[3200,256]{1,0:T(8,128)S(1)} %broadcast_multiply_fusion) | copy-start | bytes 9830404
  498.9 32.8 %copy-start.4 = (f32[3200,256]{1,0:T(8,128)S(1)}, f32[3200,256]{1,0:T(8,128)}, u32[]{:S(2)}) copy-start(f32[3200,256]{1,0:T(8,128)} %all-gather.5.cloned.1.call-done) | copy-start | bytes 9830404
  531.7 34.2 %copy-start.1 = (f32[3200,256]{1,0:T(8,128)S(1)}, f32[3200,256]{1,0:T(8,128)}, u32[]{:S(2)}) copy-start(f32[3200,256]{1,0:T(8,128)} %param.9) | copy-start | bytes 9830404
Sparse Core Ops, SparseCore 0:
  9.8 129.4 all-gather.2
  197.7 60.4 all-reduce.3
  262.9 42.0 all-reduce.5
  404.2 44.9 reduce-scatter.1
  450.9 45.7 all-gather.4
